TPU v7x, 32 devices: a whole 2x2x4 slice. The times are simulated.
32 devices in a mesh: ctx: 8 (over y, x, core), ch: 4 (over z).
Axes of the slice: x: 2, y: 2, z: 4, core: 2. Of those that a mesh axis runs over, the one named last changes fastest.
Arguments:
- queries: bfloat16 [8192, 2048], P('ch', 'ctx'), may hold values from -6 to 6
- keys: bfloat16 [8192, 2048], P('ch', 'ctx'), may hold values from -6 to 6
- values: bfloat16 [8192, 2048], P('ch', 'ctx'), may hold values from -6 to 6
- short_taps: float32 [3, 7, 8192], P(None, None, 'ch'), may hold values from -2 to 2
- long_filter: bfloat16 [4, 2048, 2048], P('ch', 'ctx'), may hold values from -1.5 to 1.5
- skip_gain: float32 [4, 2048], P('ch', 'ctx'), may hold values from 0.5 to 1.5
Outputs:
- mixed: bfloat16 [8192, 2048], P('ch', 'ctx')
All inputs are finite; a program needn't handle non-finite values.
Results may differ from a plain program's by a relative error of at most 0.01.
Values may be sent and summed in bfloat16 or wider, within the bound.
A program may use at most 64 MiB of HBM per device.

v0:
```python
import math
import jax
import jax.numpy as jnp
from jax import lax
from jax.sharding import PartitionSpec as P

HIGH = lax.Precision.HIGHEST


def passed_along(value, axis, by):
    peers = lax.axis_size(axis)
    pairs = [(i, i + by) for i in range(peers) if 0 <= i + by < peers]
    return lax.ppermute(value, axis, pairs)


def short_conv(extended, taps, length):
    rim = taps.shape[0] - 1
    total = jnp.zeros((extended.shape[0], length), jnp.float32)
    for shift_j in range(taps.shape[0]):
        total = total + taps[shift_j][:, None] * extended[:, rim - shift_j : rim - shift_j + length]
    return total


def split_table(table):
    table_head = table.astype(jnp.bfloat16)
    table_rest = (table - table_head.astype(jnp.float32)).astype(jnp.bfloat16)
    return (table_head, table_rest)


def long_conv(gated, filters, skips):
    channels, length = gated.shape
    size = 2 * length
    cols = 128
    rows = size // cols
    half = rows // 2
    two_pi = 2.0 * math.pi
    row_idx = jnp.arange(rows, dtype=jnp.int32)
    half_idx = jnp.arange(half, dtype=jnp.int32)
    col_idx = jnp.arange(cols, dtype=jnp.int32)
    angle_rows = two_pi * (row_idx[:, None] * half_idx[None, :] % rows).astype(jnp.float32) / rows
    cos_rows, sin_rows = (jnp.cos(angle_rows), jnp.sin(angle_rows))
    cos_head, cos_rest = split_table(cos_rows)
    sin_head, sin_rest = split_table(sin_rows)
    angle_twist = two_pi * (row_idx[:, None] * col_idx[None, :]).astype(jnp.float32) / size
    cos_twist, sin_twist = (jnp.cos(angle_twist), jnp.sin(angle_twist))
    angle_cols = two_pi * (col_idx[:, None] * col_idx[None, :] % cols).astype(jnp.float32) / cols
    cos_cols, sin_cols = (jnp.cos(angle_cols), jnp.sin(angle_cols))

    def first_section(table_head, table_rest, shaped):
        return jnp.einsum(
            "ka,cab->ckb", table_head, shaped, preferred_element_type=jnp.float32
        ) + jnp.einsum("ka,cab->ckb", table_rest, shaped, preferred_element_type=jnp.float32)

    def forward(signal):
        blocks = signal.shape[0]
        shaped = signal.reshape(blocks, half, cols)
        first_re = first_section(cos_head, cos_rest, shaped)
        first_im = -first_section(sin_head, sin_rest, shaped)
        twist_re = first_re * cos_twist + first_im * sin_twist
        twist_im = first_im * cos_twist - first_re * sin_twist
        out_re = jnp.einsum("ckb,bm->ckm", twist_re, cos_cols, precision=HIGH) + jnp.einsum(
            "ckb,bm->ckm", twist_im, sin_cols, precision=HIGH
        )
        out_im = jnp.einsum("ckb,bm->ckm", twist_im, cos_cols, precision=HIGH) - jnp.einsum(
            "ckb,bm->ckm", twist_re, sin_cols, precision=HIGH
        )
        return (out_re, out_im)

    def inverse(spec_re, spec_im):
        blocks = spec_re.shape[0]
        back_re = jnp.einsum("ckm,mb->ckb", spec_re, cos_cols, precision=HIGH) - jnp.einsum(
            "ckm,mb->ckb", spec_im, sin_cols, precision=HIGH
        )
        back_im = jnp.einsum("ckm,mb->ckb", spec_im, cos_cols, precision=HIGH) + jnp.einsum(
            "ckm,mb->ckb", spec_re, sin_cols, precision=HIGH
        )
        turn_re = back_re * cos_twist - back_im * sin_twist
        turn_im = back_re * sin_twist + back_im * cos_twist
        result = jnp.einsum("ka,ckb->cab", cos_rows, turn_re, precision=HIGH) - jnp.einsum(
            "ka,ckb->cab", sin_rows, turn_im, precision=HIGH
        )
        return (result / size).reshape(blocks, length)

    block = math.gcd(channels, 16)
    count = channels // block

    def one_block(triple):
        sig, filt, gain = triple
        sig_re, sig_im = forward(sig)
        filt_re, filt_im = forward(filt)
        prod_re = sig_re * filt_re - sig_im * filt_im
        prod_im = sig_re * filt_im + sig_im * filt_re
        return inverse(prod_re, prod_im) + gain[:, None] * sig.astype(jnp.float32)

    outcome = lax.map(
        one_block,
        (
            gated.reshape(count, block, length),
            filters.reshape(count, block, length),
            skips.reshape(count, block),
        ),
    )
    return outcome.reshape(channels, length).astype(jnp.bfloat16)


def gate_product(first, second):
    return (first.astype(jnp.float32) * second.astype(jnp.float32)).astype(jnp.bfloat16)


def local(queries, keys, values, short_taps, long_filter, skip_gain):
    width, tok_local = queries.shape
    rim = short_taps.shape[1] - 1
    stacked = jnp.stack(
        [queries[:, tok_local - rim :], keys[:, tok_local - rim :], values[:, tok_local - rim :]]
    )
    before = passed_along(stacked, "ctx", 1)

    def extend_home(source, which):
        return jnp.concatenate([before[which], source], axis=1).astype(jnp.float32)

    q_short = short_conv(extend_home(queries, 0), short_taps[0], tok_local).astype(jnp.bfloat16)
    gated = (
        short_conv(extend_home(keys, 1), short_taps[1], tok_local)
        * short_conv(extend_home(values, 2), short_taps[2], tok_local)
    ).astype(jnp.bfloat16)
    g_owned = lax.all_to_all(gated, "ctx", split_axis=0, concat_axis=1, tiled=True)
    outgoing = long_conv(g_owned, long_filter[0], skip_gain[0])
    returned = lax.all_to_all(outgoing, "ctx", split_axis=1, concat_axis=0, tiled=True)
    return gate_product(q_short, returned)


def solution(mesh):
    placed = (
        P("ch", "ctx"),
        P("ch", "ctx"),
        P("ch", "ctx"),
        P(None, None, "ch"),
        P("ch", "ctx", None),
        P("ch", "ctx"),
    )
    return jax.shard_map(
        local, mesh=mesh, in_specs=placed, out_specs=P("ch", "ctx"), check_vma=False
    )
```

profile of v0, /device:TPU:0, one launch (start us, length us, event | category | flops | bytes accessed | tf_op | source)
XLA Modules:
  0.0 269.8 jit_solution(2288781871409935307)
XLA Ops:
  0.0 1.3 slice.190
  1.6 1.3 slice.191
  3.5 2.4 collective-permute-start
  6.1 0.8 collective-permute-done
  7.5 1.3 maximum_convert_fusion.1
  8.8 11.8 %fusion.204 = bf16[2048,256]{1,0:T(8,128)(2,1)} fusion(f32[2048,262]{1,0:T(8,128)S(1)} %get-tuple-element.288, f32[2048,262]{1,0:T(8,128)S(1)} %get-tuple-element.287, f32[2048]{0:T(1024)S(1)} %bitcast.245, f32[2048]{0:T(1024)S(1)} %bitcast.244, f32[2048]{0:T(1024)S(1)} %bitcast.233, f32[2048]{0:T(1024)S(1)} %bitcast.234, f32[2048]{0:T(1024)S(1)} %bitcast.235, ...), kind=kLoop, calls=%fused_computation.203 | loop fusion | flops 14680064 | bytes 30523392 | tf_op jit(solution)/shard_map/convert_element_type | solution.py:125
  20.6 7.9 %all-to-all-start = ((bf16[8,256,256]{2,1,0:T(8,128)(2,1)}), bf16[8,256,256]{2,1,0:T(8,128)(2,1)S(1)}, u32[]{:S(2)}, u32[]{:S(2)}) async-start(bf16[8,256,256]{2,1,0:T(8,128)(2,1)} %bitcast.27), calls=%async_computation | async-start | bytes 2097152 | tf_op jit(solution)/shard_map/all_to_all | solution.py:126
  29.1 0.7 reduce.3
  29.9 14.0 %all-to-all-done = bf16[8,256,256]{2,1,0:T(8,128)(2,1)S(1)} async-done(((bf16[8,256,256]{2,1,0:T(8,128)(2,1)}), bf16[8,256,256]{2,1,0:T(8,128)(2,1)S(1)}, u32[]{:S(2)}, u32[]{:S(2)}) %all-to-all-start) | async-done | bytes 1048608 | tf_op jit(solution)/shard_map/all_to_all | solution.py:126
  45.0 195.2 %while.12 = (s32[]{:T(128)}, bf16[16,16,2048]{2,1,0:T(8,128)(2,1)}, bf16[16,16,2048]{2,1,0:T(8,128)(2,1)S(1)}, bf16[16,16,2048]{2,1,0:T(8,128)(2,1)}, f32[16,16]{1,0:T(8,128)S(1)}, /*index=5*/s32[]{:T(128)}) while((s32[]{:T(128)}, bf16[16,16,2048]{2,1,0:T(8,128)(2,1)}, bf16[16,16,2048]{2,1,0:T(8,128)(2,1)S(1)}, ...), condition=%wide.region_1.2_spmd.clone.clone, body=%wide.region_0.1_spmd.clone.clone.sunk | while | flops 1256058880 | bytes 17597196 | solution.py:95
  45.1 0.9 dynamic-slice_bitcast_fusion.3
  52.6 0.6 multiply_subtract_fusion.16
  56.5 0.7 add_dynamic-update-slice_fusion.2
  57.2 0.8 dynamic-slice_bitcast_fusion.3
  64.8 0.7 multiply_subtract_fusion.16
  68.7 0.7 add_dynamic-update-slice_fusion.2
  69.5 0.8 dynamic-slice_bitcast_fusion.3
  80.9 0.7 add_dynamic-update-slice_fusion.2
  81.6 0.8 dynamic-slice_bitcast_fusion.3
  89.2 0.7 multiply_subtract_fusion.16
  93.1 0.7 add_dynamic-update-slice_fusion.2
  93.8 0.8 dynamic-slice_bitcast_fusion.3
  101.4 0.6 multiply_subtract_fusion.16
  105.3 0.7 add_dynamic-update-slice_fusion.2
  106.0 0.8 dynamic-slice_bitcast_fusion.3
  113.6 0.7 multiply_subtract_fusion.16
  117.5 0.7 add_dynamic-update-slice_fusion.2
  118.2 0.8 dynamic-slice_bitcast_fusion.3
  125.8 0.6 multiply_subtract_fusion.16
  129.7 0.7 add_dynamic-update-slice_fusion.2
  130.4 0.8 dynamic-slice_bitcast_fusion.3
  138.0 0.7 multiply_subtract_fusion.16
  141.9 0.7 add_dynamic-update-slice_fusion.2
  142.6 0.8 dynamic-slice_bitcast_fusion.3
  150.2 0.6 multiply_subtract_fusion.16
  154.1 0.7 add_dynamic-update-slice_fusion.2
  154.8 0.8 dynamic-slice_bitcast_fusion.3
  162.4 0.7 multiply_subtract_fusion.16
  166.3 0.7 add_dynamic-update-slice_fusion.2
  167.0 0.8 dynamic-slice_bitcast_fusion.3
  174.6 0.6 multiply_subtract_fusion.16
  178.5 0.7 add_dynamic-update-slice_fusion.2
  179.2 0.8 dynamic-slice_bitcast_fusion.3
  186.8 0.7 multiply_subtract_fusion.16
  190.7 0.7 add_dynamic-update-slice_fusion.2
  191.4 0.8 dynamic-slice_bitcast_fusion.3
  199.0 0.6 multiply_subtract_fusion.16
  202.9 0.7 add_dynamic-update-slice_fusion.2
  203.6 0.8 dynamic-slice_bitcast_fusion.3
  211.2 0.7 multiply_subtract_fusion.16
  215.1 0.7 add_dynamic-update-slice_fusion.2
  215.8 0.8 dynamic-slice_bitcast_fusion.3
  223.4 0.6 multiply_subtract_fusion.16
  227.3 0.7 add_dynamic-update-slice_fusion.2
  228.0 0.8 dynamic-slice_bitcast_fusion.3
  235.6 0.7 multiply_subtract_fusion.16
  239.5 0.7 add_dynamic-update-slice_fusion.2
  240.2 1.5 copy.29
  241.8 1.2 copy.23
  242.9 4.2 %all-to-all-start.1 = ((bf16[256,8,256]{2,0,1:T(8,128)(2,1)}), bf16[256,8,256]{2,0,1:T(8,128)(2,1)}, u32[]{:S(2)}, u32[]{:S(2)}) async-start(bf16[256,8,256]{2,0,1:T(8,128)(2,1)} %copy.23), calls=%async_computation.1 | async-start | bytes 2097152 | tf_op jit(solution)/shard_map/all_to_all | solution.py:128
  247.2 1.1 copy.19
  248.3 2.0 maximum_convert_fusion
  250.3 12.3 %all-to-all-done.1 = bf16[256,8,256]{2,0,1:T(8,128)(2,1)} async-done(((bf16[256,8,256]{2,0,1:T(8,128)(2,1)}), bf16[256,8,256]{2,0,1:T(8,128)(2,1)}, u32[]{:S(2)}, u32[]{:S(2)}) %all-to-all-start.1) | async-done | bytes 1048608 | tf_op jit(solution)/shard_map/all_to_all | solution.py:128
  262.6 7.2 %fusion.223 = bf16[2048,256]{1,0:T(8,128)(2,1)} fusion(f32[2048,262]{1,0:T(8,128)S(1)} %maximum_convert_fusion, f32[2048]{0:T(1024)S(1)} %bitcast.225, f32[2048]{0:T(1024)S(1)} %bitcast.226, f32[2048]{0:T(1024)S(1)} %bitcast.227, f32[2048]{0:T(1024)S(1)} %bitcast.228, f32[2048]{0:T(1024)S(1)} %bitcast.229, f32[2048]{0:T(1024)S(1)} %bitcast.230, ...), kind=kLoop, calls=%fused_computation.243 | loop fusion | flops 9437184 | bytes 16834560 | tf_op jit(solution)/shard_map/convert_element_type | solution.py:107
  (440 shorter events, 160.5 us)
Async XLA Ops:
  0.0 3.1 %copy-start = (bf16[2048,256]{1,0:T(8,128)(2,1)S(1)}, bf16[2048,256]{1,0:T(8,128)(2,1)}, u32[]{:S(2)}) copy-start(bf16[2048,256]{1,0:T(8,128)(2,1)} %param.10) | copy-start | bytes 3145732
  1.3 4.6 %copy-start.2 = (f32[3,7,2048]{2,1,0:T(8,128)S(1)}, f32[3,7,2048]{2,1,0:T(8,128)}, u32[]{:S(2)}) copy-start(f32[3,7,2048]{2,1,0:T(8,128)} %param.11) | copy-start | bytes 516100
  2.8 4.7 %copy-start.1 = (bf16[2048,256]{1,0:T(8,128)(2,1)S(1)}, bf16[2048,256]{1,0:T(8,128)(2,1)}, u32[]{:S(2)}) copy-start(bf16[2048,256]{1,0:T(8,128)(2,1)} %param.9) | copy-start | bytes 3145732
  3.5 3.3 %collective-permute-start = (bf16[3,2048,6]{1,2,0:T(8,128)(2,1)S(1)}, bf16[3,2048,6]{1,2,0:T(8,128)(2,1)S(1)}, u32[]{:S(2)}, u32[]{:S(2)}) collective-permute-start(bf16[3,2048,6]{1,2,0:T(8,128)(2,1)S(1)} %pad_maximum_fusion), channel_id=1, source_target_pairs={{0,4},{4,8},{8,12},{12,16},{16,20},{20,24},{24,28},{1,5},{5,9},{9,... | collective-permute-start | bytes 221192 | tf_op jit(solution)/shard_map/ppermute | solution.py:13
  20.6 8.5 %copy-start.3 = (f32[1,256]{1,0:T(1,128)S(1)}, f32[1,256]{1,0:T(1,128)}, u32[]{:S(2)}) copy-start(f32[1,256]{1,0:T(1,128)} %param.13) | copy-start | bytes 3076
  20.6 23.3 %all-to-all-start = ((bf16[8,256,256]{2,1,0:T(8,128)(2,1)}), bf16[8,256,256]{2,1,0:T(8,128)(2,1)S(1)}, u32[]{:S(2)}, u32[]{:S(2)}) async-start(bf16[8,256,256]{2,1,0:T(8,128)(2,1)} %bitcast.27), calls=%async_computation | async-start | bytes 2097152 | tf_op jit(solution)/shard_map/all_to_all | solution.py:126
  242.9 19.6 %all-to-all-start.1 = ((bf16[256,8,256]{2,0,1:T(8,128)(2,1)}), bf16[256,8,256]{2,0,1:T(8,128)(2,1)}, u32[]{:S(2)}, u32[]{:S(2)}) async-start(bf16[256,8,256]{2,0,1:T(8,128)(2,1)} %copy.23), calls=%async_computation.1 | async-start | bytes 2097152 | tf_op jit(solution)/shard_map/all_to_all | solution.py:128
where the time goes:
time: 271 us; the launch traced here: 270 us
  matrix products  164 us (61%)
  other arithmetic  35.8 us (13%)
  waiting for transfers between devices  27 us (10%)
  local copies, waits for them, and re-layouts  24.4 us (9%)
  starting transfers between devices  14.6 us (5%)
  loops' own time  3.38 us (1%)
    dot_general x32, matrix products, forward(): jnp.einsum('ckb,bm->ckm', twist_re, sin_cols, precision=HIGH)  20.2 us
    dot_general x32, matrix products, forward(): jnp.einsum('ckb,bm->ckm', twist_im, sin_cols, precision=HIGH)  19.7 us
    dot_general x32, matrix products, forward(): jnp.einsum('ckb,bm->ckm', twist_im, cos_cols, precision=HIGH)  19.5 us
    dot_general x32, matrix products, forward(): jnp.einsum('ckb,bm->ckm', twist_re, cos_cols, precision=HIGH)  19.5 us
    dot_general x64, matrix products, first_section(): jnp.einsum('ka,cab->ckb', table_rest, shaped, preferred_element_type=jnp....  17.9 us
    dot_general x64, matrix products, first_section(): jnp.einsum('ka,cab->ckb', table_head, shaped, preferred_element_type=jnp....  17.5 us
    all_to_all x1, waiting for transfers between devices, local(): lax.all_to_all(gated, 'ctx', split_axis=0, concat_axis=1, tiled=True)  14 us
    while x48, local copies, waits for them, and re-layouts  14 us
  transfers between devices with their start and end apart: 3, of which 3 were waited for; matrix products, arithmetic and copies ran while one was open for 2% of the time, Pallas kernels for 0%

commit v1 on v0

--- a/solution.py
+++ b/solution.py
@@ -3,6 +3,7 @@
 import jax.numpy as jnp
 from jax import lax
 from jax.sharding import PartitionSpec as P
+from jax.lax import axis_index, ppermute, psum
 
 HIGH = lax.Precision.HIGHEST
 
@@ -123,7 +124,21 @@
         short_conv(extend_home(keys, 1), short_taps[1], tok_local)
         * short_conv(extend_home(values, 2), short_taps[2], tok_local)
     ).astype(jnp.bfloat16)
-    g_owned = lax.all_to_all(gated, "ctx", split_axis=0, concat_axis=1, tiled=True)
+    y2 = psum(1, "ctx")
+    b_next, local_out = (y2, axis_index("ctx"))
+    u_next = gated.shape[0] // b_next
+    arr_out = list(gated.shape)
+    arr_out[0] = u_next
+    value_now = arr_out[1]
+    arr_out[1] = value_now * b_next
+    g_owned = jnp.zeros(arr_out, gated.dtype)
+    for c in [*range(b_next)]:
+        long_array = lax.dynamic_slice_in_dim(gated, (local_out ^ c) * u_next, u_next, axis=0)
+        if c:
+            long_array = ppermute(long_array, "ctx", [(num, num ^ c) for num in range(b_next)])
+        g_owned = lax.dynamic_update_slice_in_dim(
+            g_owned, long_array, (local_out ^ c) * value_now, axis=1
+        )
     outgoing = long_conv(g_owned, long_filter[0], skip_gain[0])
     returned = lax.all_to_all(outgoing, "ctx", split_axis=1, concat_axis=0, tiled=True)
     return gate_product(q_short, returned)

time: 271 us -> 257 us (0.948)
  other arithmetic: 35.8 us -> 25 us
  waiting for transfers between devices: 27 us -> 22.6 us
  starting transfers between devices: 14.6 us -> 17.5 us
    all_to_all x1 -> x0, waiting for transfers between devices: 14 us -> none  [local(): lax.all_to_all(gated, 'ctx', split_axis=0, concat_axis=1, tiled=True)]
    ppermute x0 -> x7, starting transfers between devices: none -> 10.9 us  [local(): ppermute(long_array, 'ctx', [(num, num ^ c) for num in range(b_next)])]
    dynamic_update_slice x16, other arithmetic: 11.5 us -> 1.36 us  [long_conv(): lax.map(one_block, (gated.reshape(count, block, length), filters.reshape(...]
    ppermute x0 -> x7, waiting for transfers between devices: none -> 9.61 us  [local(): ppermute(long_array, 'ctx', [(num, num ^ c) for num in range(b_next)])]
    all_to_all x1 -> x0, starting transfers between devices: 7.94 us -> none  [local(): lax.all_to_all(gated, 'ctx', split_axis=0, concat_axis=1, tiled=True)]
  transfers between devices with their start and end apart: 3 -> 9, of which waited for: 3 -> 5; matrix products, arithmetic and copies ran while one was open for 2% -> 2% of each run, Pallas kernels for 0% -> 0%
where the time goes in v1:
time: 257 us; the launch traced here: 256 us
  matrix products  165 us (64%)
  other arithmetic  25 us (10%)
  waiting for transfers between devices  22.6 us (9%)
  local copies, waits for them, and re-layouts  22.4 us (9%)
  starting transfers between devices  17.5 us (7%)
  loops' own time  3.65 us (1%)
    dot_general x32, matrix products, forward(): jnp.einsum('ckb,bm->ckm', twist_re, sin_cols, precision=HIGH)  20.2 us
    dot_general x32, matrix products, forward(): jnp.einsum('ckb,bm->ckm', twist_im, sin_cols, precision=HIGH)  19.8 us
    dot_general x32, matrix products, forward(): jnp.einsum('ckb,bm->ckm', twist_im, cos_cols, precision=HIGH)  19.5 us
    dot_general x32, matrix products, forward(): jnp.einsum('ckb,bm->ckm', twist_re, cos_cols, precision=HIGH)  19.5 us
    dot_general x64, matrix products, first_section(): jnp.einsum('ka,cab->ckb', table_rest, shaped, preferred_element_type=jnp....  17.9 us
    dot_general x64, matrix products, first_section(): jnp.einsum('ka,cab->ckb', table_head, shaped, preferred_element_type=jnp....  17.5 us
    while x48, local copies, waits for them, and re-layouts  14 us
    all_to_all x1, waiting for transfers between devices, local(): lax.all_to_all(outgoing, 'ctx', split_axis=1, concat_axis=0, tiled=True)  12.3 us
  transfers between devices with their start and end apart: 9, of which 5 were waited for; matrix products, arithmetic and copies ran while one was open for 2% of the time, Pallas kernels for 0%

profile of v1, /device:TPU:0, one launch (start us, length us, event | category | flops | bytes accessed | tf_op | source)
XLA Modules:
  0.0 256.0 jit_solution(15116046127427045337)
XLA Ops:
  0.0 1.3 slice.190
  1.6 1.3 slice.191
  3.5 2.4 collective-permute-start
  6.2 0.7 collective-permute-done
  7.5 1.3 maximum_convert_fusion.1
  8.8 11.3 %fusion.204 = bf16[2048,256]{1,0:T(8,128)(2,1)S(1)} fusion(f32[2048,262]{1,0:T(8,128)S(1)} %get-tuple-element.296, f32[2048,262]{1,0:T(8,128)S(1)} %get-tuple-element.295, f32[2048]{0:T(1024)S(1)} %bitcast.246, f32[2048]{0:T(1024)S(1)} %bitcast.245, f32[2048]{0:T(1024)S(1)} %bitcast.234, f32[2048]{0:T(1024)S(1)} %bitcast.235, f32[2048]{0:T(1024)S(1)} %bitcast.236, ...), kind=kLoop, calls=%fused_computation.203 | loop fusion | flops 14680064 | bytes 30523392 | tf_op jit(solution)/shard_map/convert_element_type | solution.py:126
  20.3 3.4 %collective-permute-start.1 = (bf16[256,256]{1,0:T(8,128)(2,1)S(1)}, bf16[256,256]{1,0:T(8,128)(2,1)S(1)}, u32[]{:S(2)}, u32[]{:S(2)}) collective-permute-start(bf16[256,256]{1,0:T(8,128)(2,1)S(1)} %get-tuple-element.269), channel_id=1, source_target_pairs={{0,4},{4,0},{8,12},{12,8},{16,20},{20,16},{24,28},{28,24},{1,5},{5... | collective-permute-start | bytes 393224 | tf_op jit(solution)/shard_map/ppermute | solution.py:138
  23.7 2.4 collective-permute-start.2
  27.3 2.7 %collective-permute-start.4 = (bf16[256,256]{1,0:T(8,128)(2,1)S(1)}, bf16[256,256]{1,0:T(8,128)(2,1)S(1)}, u32[]{:S(2)}, u32[]{:S(2)}) collective-permute-start(bf16[256,256]{1,0:T(8,128)(2,1)S(1)} %get-tuple-element.266), channel_id=1, source_target_pairs={{0,16},{4,20},{8,24},{12,28},{16,0},{20,4},{24,8},{28,12},{1,17},{... | collective-permute-start | bytes 393224 | tf_op jit(solution)/shard_map/ppermute | solution.py:138
  29.9 1.7 collective-permute-start.6
  31.7 0.7 collective-permute-start.7
  32.7 6.6 %collective-permute-done.4 = bf16[256,256]{1,0:T(8,128)(2,1)S(1)} collective-permute-done((bf16[256,256]{1,0:T(8,128)(2,1)S(1)}, bf16[256,256]{1,0:T(8,128)(2,1)S(1)}, u32[]{:S(2)}, u32[]{:S(2)}) %collective-permute-start.4) | collective-permute-done | bytes 131104 | tf_op jit(solution)/shard_map/ppermute | solution.py:138
  39.3 2.7 %collective-permute-done.5 = bf16[256,256]{1,0:T(8,128)(2,1)S(1)} collective-permute-done((bf16[256,256]{1,0:T(8,128)(2,1)S(1)}, bf16[256,256]{1,0:T(8,128)(2,1)S(1)}, u32[]{:S(2)}, u32[]{:S(2)}) %collective-permute-start.5) | collective-permute-done | bytes 131104 | tf_op jit(solution)/shard_map/ppermute | solution.py:138
  42.1 185.5 %while.12 = (s32[]{:T(128)}, bf16[16,16,2048]{2,1,0:T(8,128)(2,1)S(1)}, bf16[16,16,2048]{2,1,0:T(8,128)(2,1)S(1)}, bf16[16,16,2048]{2,1,0:T(8,128)(2,1)}, f32[16,16]{1,0:T(8,128)S(1)}, /*index=5*/s32[]{:T(128)}) while((s32[]{:T(128)}, bf16[16,16,2048]{2,1,0:T(8,128)(2,1)S(1)}, bf16[16,16,2048]{2,1,0:T(8,128)(2,1)S(1)}, ...), condition=%wide.region_1.2_spmd.clone.clone, body=%wide.region_0.1_spmd.clone.clone.sunk | while | flops 1256058880 | bytes 17597136 | solution.py:96
  42.1 0.9 dynamic-slice_bitcast_fusion.3
  49.7 0.7 multiply_subtract_fusion.16
  53.7 0.9 dynamic-slice_bitcast_fusion.3
  56.4 0.6 convolution_add_fusion.11
  61.3 0.7 multiply_subtract_fusion.16
  65.3 0.9 dynamic-slice_bitcast_fusion.3
  68.0 0.6 convolution_add_fusion.11
  72.9 0.7 multiply_subtract_fusion.16
  76.9 0.9 dynamic-slice_bitcast_fusion.3
  79.6 0.6 convolution_add_fusion.11
  84.5 0.7 multiply_subtract_fusion.16
  88.5 0.9 dynamic-slice_bitcast_fusion.3
  91.2 0.6 convolution_add_fusion.11
  96.1 0.7 multiply_subtract_fusion.16
  100.1 0.9 dynamic-slice_bitcast_fusion.3
  102.8 0.6 convolution_add_fusion.11
  107.7 0.7 multiply_subtract_fusion.16
  111.7 0.9 dynamic-slice_bitcast_fusion.3
  114.4 0.6 convolution_add_fusion.11
  119.3 0.7 multiply_subtract_fusion.16
  123.3 0.9 dynamic-slice_bitcast_fusion.3
  126.0 0.6 convolution_add_fusion.11
  130.9 0.7 multiply_subtract_fusion.16
  134.9 0.9 dynamic-slice_bitcast_fusion.3
  137.6 0.6 convolution_add_fusion.11
  142.5 0.7 multiply_subtract_fusion.16
  146.5 0.9 dynamic-slice_bitcast_fusion.3
  149.2 0.6 convolution_add_fusion.11
  154.1 0.7 multiply_subtract_fusion.16
  158.1 0.9 dynamic-slice_bitcast_fusion.3
  160.8 0.6 convolution_add_fusion.11
  165.7 0.7 multiply_subtract_fusion.16
  169.7 0.9 dynamic-slice_bitcast_fusion.3
  177.3 0.7 multiply_subtract_fusion.16
  181.3 0.9 dynamic-slice_bitcast_fusion.3
  184.0 0.6 convolution_add_fusion.11
  188.9 0.7 multiply_subtract_fusion.16
  192.9 0.9 dynamic-slice_bitcast_fusion.3
  200.5 0.7 multiply_subtract_fusion.16
  204.5 0.9 dynamic-slice_bitcast_fusion.3
  207.2 0.6 convolution_add_fusion.11
  212.1 0.7 multiply_subtract_fusion.16
  216.1 0.9 dynamic-slice_bitcast_fusion.3
  223.7 0.7 multiply_subtract_fusion.16
  228.0 1.2 copy.14
  229.1 4.2 %all-to-all-start = ((bf16[256,8,256]{2,0,1:T(8,128)(2,1)}), bf16[256,8,256]{2,0,1:T(8,128)(2,1)}, u32[]{:S(2)}, u32[]{:S(2)}) async-start(bf16[256,8,256]{2,0,1:T(8,128)(2,1)} %copy.14), calls=%async_computation | async-start | bytes 2097152 | tf_op jit(solution)/shard_map/all_to_all | solution.py:143
  233.4 1.1 copy.11
  234.5 2.0 maximum_convert_fusion
  236.5 12.3 %all-to-all-done = bf16[256,8,256]{2,0,1:T(8,128)(2,1)} async-done(((bf16[256,8,256]{2,0,1:T(8,128)(2,1)}), bf16[256,8,256]{2,0,1:T(8,128)(2,1)}, u32[]{:S(2)}, u32[]{:S(2)}) %all-to-all-start) | async-done | bytes 1048608 | tf_op jit(solution)/shard_map/all_to_all | solution.py:143
  248.8 7.2 %fusion.223 = bf16[2048,256]{1,0:T(8,128)(2,1)} fusion(f32[2048,262]{1,0:T(8,128)S(1)} %maximum_convert_fusion, f32[2048]{0:T(1024)S(1)} %bitcast.226, f32[2048]{0:T(1024)S(1)} %bitcast.227, f32[2048]{0:T(1024)S(1)} %bitcast.228, f32[2048]{0:T(1024)S(1)} %bitcast.229, f32[2048]{0:T(1024)S(1)} %bitcast.230, f32[2048]{0:T(1024)S(1)} %bitcast.231, ...), kind=kLoop, calls=%fused_computation.243 | loop fusion | flops 9437184 | bytes 16834560 | tf_op jit(solution)/shard_map/convert_element_type | solution.py:108
  (459 shorter events, 154.1 us)
Async XLA Ops:
  0.0 3.1 %copy-start = (bf16[2048,256]{1,0:T(8,128)(2,1)S(1)}, bf16[2048,256]{1,0:T(8,128)(2,1)}, u32[]{:S(2)}) copy-start(bf16[2048,256]{1,0:T(8,128)(2,1)} %param.10) | copy-start | bytes 3145732
  1.3 4.6 %copy-start.2 = (f32[3,7,2048]{2,1,0:T(8,128)S(1)}, f32[3,7,2048]{2,1,0:T(8,128)}, u32[]{:S(2)}) copy-start(f32[3,7,2048]{2,1,0:T(8,128)} %param.11) | copy-start | bytes 516100
  2.8 4.7 %copy-start.1 = (bf16[2048,256]{1,0:T(8,128)(2,1)S(1)}, bf16[2048,256]{1,0:T(8,128)(2,1)}, u32[]{:S(2)}) copy-start(bf16[2048,256]{1,0:T(8,128)(2,1)} %param.9) | copy-start | bytes 3145732
  3.5 3.3 %collective-permute-start = (bf16[3,2048,6]{1,2,0:T(8,128)(2,1)S(1)}, bf16[3,2048,6]{1,2,0:T(8,128)(2,1)S(1)}, u32[]{:S(2)}, u32[]{:S(2)}) collective-permute-start(bf16[3,2048,6]{1,2,0:T(8,128)(2,1)S(1)} %pad_maximum_fusion), channel_id=1, source_target_pairs={{0,4},{4,8},{8,12},{12,16},{16,20},{20,24},{24,28},{1,5},{5,9},{9,... | collective-permute-start | bytes 221192 | tf_op jit(solution)/shard_map/ppermute | solution.py:14
  20.1 6.5 %copy-start.3 = (f32[1,256]{1,0:T(1,128)S(1)}, f32[1,256]{1,0:T(1,128)}, u32[]{:S(2)}) copy-start(f32[1,256]{1,0:T(1,128)} %param.13) | copy-start | bytes 3076
  20.3 9.6 %collective-permute-start.1 = (bf16[256,256]{1,0:T(8,128)(2,1)S(1)}, bf16[256,256]{1,0:T(8,128)(2,1)S(1)}, u32[]{:S(2)}, u32[]{:S(2)}) collective-permute-start(bf16[256,256]{1,0:T(8,128)(2,1)S(1)} %get-tuple-element.269), channel_id=1, source_target_pairs={{0,4},{4,0},{8,12},{12,8},{16,20},{20,16},{24,28},{28,24},{1,5},{5... | collective-permute-start | bytes 393224 | tf_op jit(solution)/shard_map/ppermute | solution.py:138
  23.7 8.0 %collective-permute-start.2 = (bf16[256,256]{1,0:T(8,128)(2,1)S(1)}, bf16[256,256]{1,0:T(8,128)(2,1)S(1)}, u32[]{:S(2)}, u32[]{:S(2)}) collective-permute-start(bf16[256,256]{1,0:T(8,128)(2,1)S(1)} %get-tuple-element.268), channel_id=1, source_target_pairs={{0,8},{4,12},{8,0},{12,4},{16,24},{20,28},{24,16},{28,20},{1,9},{5... | collective-permute-start | bytes 393224 | tf_op jit(solution)/shard_map/ppermute | solution.py:138
  27.2 5.5 %collective-permute-start.3 = (bf16[256,256]{1,0:T(8,128)(2,1)S(1)}, bf16[256,256]{1,0:T(8,128)(2,1)S(1)}, u32[]{:S(2)}, u32[]{:S(2)}) collective-permute-start(bf16[256,256]{1,0:T(8,128)(2,1)S(1)} %get-tuple-element.267), channel_id=1, source_target_pairs={{0,12},{4,8},{8,4},{12,0},{16,28},{20,24},{24,20},{28,16},{1,13},{... | collective-permute-start | bytes 393224 | tf_op jit(solution)/shard_map/ppermute | solution.py:138
  27.3 12.0 %collective-permute-start.4 = (bf16[256,256]{1,0:T(8,128)(2,1)S(1)}, bf16[256,256]{1,0:T(8,128)(2,1)S(1)}, u32[]{:S(2)}, u32[]{:S(2)}) collective-permute-start(bf16[256,256]{1,0:T(8,128)(2,1)S(1)} %get-tuple-element.266), channel_id=1, source_target_pairs={{0,16},{4,20},{8,24},{12,28},{16,0},{20,4},{24,8},{28,12},{1,17},{... | collective-permute-start | bytes 393224 | tf_op jit(solution)/shard_map/ppermute | solution.py:138
  29.9 12.1 %collective-permute-start.5 = (bf16[256,256]{1,0:T(8,128)(2,1)S(1)}, bf16[256,256]{1,0:T(8,128)(2,1)S(1)}, u32[]{:S(2)}, u32[]{:S(2)}) collective-permute-start(bf16[256,256]{1,0:T(8,128)(2,1)S(1)} %get-tuple-element.265), channel_id=1, source_target_pairs={{0,20},{4,16},{8,28},{12,24},{16,4},{20,0},{24,12},{28,8},{1,21},{... | collective-permute-start | bytes 393224 | tf_op jit(solution)/shard_map/ppermute | solution.py:138
  29.9 12.1 %collective-permute-start.6 = (bf16[256,256]{1,0:T(8,128)(2,1)S(1)}, bf16[256,256]{1,0:T(8,128)(2,1)S(1)}, u32[]{:S(2)}, u32[]{:S(2)}) collective-permute-start(bf16[256,256]{1,0:T(8,128)(2,1)S(1)} %get-tuple-element.264), channel_id=1, source_target_pairs={{0,24},{4,28},{8,16},{12,20},{16,8},{20,12},{24,0},{28,4},{1,25},{... | collective-permute-start | bytes 393224 | tf_op jit(solution)/shard_map/ppermute | solution.py:138
  31.7 10.4 %collective-permute-start.7 = (bf16[256,256]{1,0:T(8,128)(2,1)S(1)}, bf16[256,256]{1,0:T(8,128)(2,1)S(1)}, u32[]{:S(2)}, u32[]{:S(2)}) collective-permute-start(bf16[256,256]{1,0:T(8,128)(2,1)S(1)} %get-tuple-element.263), channel_id=1, source_target_pairs={{0,28},{4,24},{8,20},{12,16},{16,12},{20,8},{24,4},{28,0},{1,29},{... | collective-permute-start | bytes 393224 | tf_op jit(solution)/shard_map/ppermute | solution.py:138
  229.1 19.6 %all-to-all-start = ((bf16[256,8,256]{2,0,1:T(8,128)(2,1)}), bf16[256,8,256]{2,0,1:T(8,128)(2,1)}, u32[]{:S(2)}, u32[]{:S(2)}) async-start(bf16[256,8,256]{2,0,1:T(8,128)(2,1)} %copy.14), calls=%async_computation | async-start | bytes 2097152 | tf_op jit(solution)/shard_map/all_to_all | solution.py:143
